TPU v7x, 32 devices: a whole 2x2x4 slice. The times are simulated.
32 devices in a mesh: layer: 4 (over y, x), row: 4 (over z), col: 2 (over core).
Axes of the slice: x: 2, y: 2, z: 4, core: 2. Of those that a mesh axis runs over, the one named last changes fastest.
Arguments:
- statistic: float32 [8, 7168, 7168], P('layer', 'row', 'col'), as said below
- eigenbasis: float32 [8, 7168, 1024], P('layer', 'col'), may hold values from -0.0625 to 0.0625
Outputs:
- refreshed: float32 [8, 7168, 1024], P('layer', ('row', 'col'))
Inputs may be any that keep to these rules, and one draw needn't show every extreme that they name: `statistic`: each layer's matrix is symmetric and positive definite.
All inputs are finite; a program needn't handle non-finite values.
Results may differ from a plain program's by a relative error of at most 0.00014.
Values sent between devices are 32-bit elements; how exact they have to be, the bound alone decides.
A program may use at most 192 MiB of HBM per device.

v0:
```python
import jax
import jax.numpy as jnp
from jax import lax
from jax.sharding import PartitionSpec as P


def contract(left_operand, right_operand):
    return lax.dot_general(
        left_operand,
        right_operand,
        (((0,), (0,)), ((), ())),
        precision=lax.Precision.HIGHEST,
        preferred_element_type=jnp.float32,
    )


def multiply(left_operand, right_operand):
    return jnp.dot(
        left_operand,
        right_operand,
        precision=lax.Precision.HIGHEST,
        preferred_element_type=jnp.float32,
    )


def on_device(statistic, eigenbasis):
    results = []
    for member in range(statistic.shape[0]):
        stat_layer = statistic[member]
        basis_layer = eigenbasis[member]
        row_product = lax.psum_scatter(
            multiply(stat_layer, basis_layer), "col", scatter_dimension=0, tiled=True
        )
        gram_matrix = lax.psum(contract(row_product, row_product), ("row", "col"))
        factor = jnp.linalg.cholesky(gram_matrix)
        result = lax.linalg.triangular_solve(
            factor, row_product, left_side=False, lower=True, transpose_a=True
        )
        results.append(result)
    return jnp.stack(results)


def solution(mesh):
    placed = (P("layer", "row", "col"), P("layer", "col", None))
    return jax.shard_map(
        on_device,
        mesh=mesh,
        in_specs=placed,
        out_specs=P("layer", ("row", "col"), None),
        check_vma=False,
    )
```

profile of v0, /device:TPU:0, one launch (start us, length us, event | category | flops | bytes accessed | tf_op | source)
XLA Modules:
  0.0 1133.4 jit_solution(6855643901012336946)
XLA Ops:
  6.5 89.5 %fusion.2 = f32[1792,1024]{1,0:T(8,128)} fusion(f32[2,1792,3584]{2,1,0:T(8,128)} %param.5, f32[2,3584,1024]{2,1,0:T(8,128)} %param.6), kind=kOutput, calls=%fused_computation.6 | convolution fusion | flops 78920024064 | bytes 47710208 | tf_op jit(solution)/shard_map/dot_general | solution.py:18
  96.3 89.6 %fusion = f32[1792,1024]{1,0:T(8,128)} fusion(f32[2,1792,3584]{2,1,0:T(8,128)} %param.5, f32[2,3584,1024]{2,1,0:T(8,128)} %param.6), kind=kOutput, calls=%fused_computation.4 | convolution fusion | flops 78920024064 | bytes 47710208 | tf_op jit(solution)/shard_map/dot_general | solution.py:18
  186.4 17.5 %fusion.150 = f32[1024,1024]{0,1:T(8,128)} fusion(f32[896,1024]{1,0:T(8,128)} %reduce-scatter.3.cloned.1.call-done), kind=kOutput, calls=%fused_computation.321 | convolution fusion | flops 11274289152 | bytes 7864320 | tf_op jit(solution)/shard_map/dot_general | solution.py:8
  204.9 17.5 %fusion.151 = f32[1024,1024]{0,1:T(8,128)} fusion(f32[896,1024]{1,0:T(8,128)} %reduce-scatter.5.cloned.1.call-done), kind=kOutput, calls=%fused_computation.322 | convolution fusion | flops 11274289152 | bytes 7864320 | tf_op jit(solution)/shard_map/dot_general | solution.py:8
  222.4 177.4 %all-reduce.4.cloned.1.call-done = (f32[1024,1024]{0,1:T(8,128)}, f32[1024,1024]{0,1:T(8,128)}) async-done(((f32[1024,1024]{0,1:T(8,128)}, f32[1024,1024]{0,1:T(8,128)}), (f32[1024,1024]{0,1:T(8,128)}, f32[1024,1024]{0,1:T(8,128)})) %all-reduce.4.cloned.1.call-update) | async-done | bytes 8388624 | tf_op jit(solution)/shard_map/psum | solution.py:34
  399.8 5.3 copy.4
  405.2 5.5 copy.6
  410.7 10.4 fusion.10
  423.0 11.7 %cholesky.619 = f32[128,128]{1,0:T(8,128)S(1)} custom-call(f32[128,128]{1,0:T(8,128)S(1)} %cholesky.911), custom_call_target="Cholesky" | custom-call | tf_op jit(solution)/shard_map/jit(cholesky)/cholesky | solution.py:35
  434.8 9.8 custom-call.55
  444.6 2.5 cholesky.645
  447.1 2.4 constant_dynamic-update-slice_fusion.63
  451.0 11.9 %cholesky.638 = f32[128,128]{1,0:T(8,128)S(1)} custom-call(f32[128,128]{1,0:T(8,128)S(1)} %cholesky.915), custom_call_target="Cholesky" | custom-call | tf_op jit(solution)/shard_map/jit(cholesky)/cholesky | solution.py:35
  464.8 9.8 custom-call.56
  478.0 11.7 %cholesky.659 = f32[128,128]{1,0:T(8,128)S(1)} custom-call(f32[128,128]{1,0:T(8,128)S(1)} %cholesky.920), custom_call_target="Cholesky" | custom-call | tf_op jit(solution)/shard_map/jit(cholesky)/cholesky | solution.py:35
  491.0 9.8 custom-call.57
  501.9 2.8 convolution_subtract_fusion.15
  504.7 11.7 %cholesky.678 = f32[128,128]{1,0:T(8,128)S(1)} custom-call(f32[128,128]{1,0:T(8,128)S(1)} %cholesky.925), custom_call_target="Cholesky" | custom-call | tf_op jit(solution)/shard_map/jit(cholesky)/cholesky | solution.py:35
  517.7 9.8 custom-call.58
  531.0 11.7 %cholesky.697 = f32[128,128]{1,0:T(8,128)S(1)} custom-call(f32[128,128]{1,0:T(8,128)S(1)} %cholesky.930), custom_call_target="Cholesky" | custom-call | tf_op jit(solution)/shard_map/jit(cholesky)/cholesky | solution.py:35
  543.9 10.0 custom-call.59
  557.2 11.7 %cholesky.716 = f32[128,128]{1,0:T(8,128)S(1)} custom-call(f32[128,128]{1,0:T(8,128)S(1)} %cholesky.935), custom_call_target="Cholesky" | custom-call | tf_op jit(solution)/shard_map/jit(cholesky)/cholesky | solution.py:35
  570.3 9.8 custom-call.60
  583.1 11.9 %cholesky.735 = f32[128,128]{1,0:T(8,128)S(1)} custom-call(f32[128,128]{1,0:T(8,128)S(1)} %cholesky.940), custom_call_target="Cholesky" | custom-call | tf_op jit(solution)/shard_map/jit(cholesky)/cholesky | solution.py:35
  596.3 9.8 custom-call.61
  608.8 11.7 %cholesky.752 = f32[128,128]{1,0:T(8,128)S(1)} custom-call(f32[128,128]{1,0:T(8,128)S(1)} %convolution_subtract_fusion.23), custom_call_target="Cholesky" | custom-call | tf_op jit(solution)/shard_map/jit(cholesky)/cholesky | solution.py:35
  626.6 4.8 select_select_fusion.1
  631.5 22.8 %while.4 = (s32[]{:T(128)}, f32[1024,1024]{1,0:T(8,128)}, s32[8,2]{0,1:T(2,128)S(1)}, f32[8,128,128]{2,1,0:T(8,128)S(1)}, s32[]{:T(128)}) while((s32[]{:T(128)}, f32[1024,1024]{1,0:T(8,128)}, s32[8,2]{0,1:T(2,128)S(1)}, f32[8,128,128]{2,1,0:T(8,128)S(1)}, s32[]{:T(128)}) %tuple.114), condition=%wide.while_cond, body=%wide.while_body.sunk | while | flops 2 | bytes 131181 | solution.py:36
  654.3 79.0 %custom-call.62 = f32[8,128,128]{1,2,0:T(8,128)S(1)} custom-call(f32[8,128,128]{2,1,0:T(8,128)S(1)} %get-tuple-element.21), custom_call_target="InvertDiagBlocksLowerTriangular" | custom-call | tf_op jit(solution)/shard_map/triangular_solve/custom-call.7 | solution.py:36
  734.2 11.7 %cholesky.767 = f32[128,128]{1,0:T(8,128)S(1)} custom-call(f32[128,128]{1,0:T(8,128)S(1)} %cholesky.944), custom_call_target="Cholesky" | custom-call | tf_op jit(solution)/shard_map/jit(cholesky)/cholesky | solution.py:35
  745.9 9.8 custom-call.63
  755.7 2.5 cholesky.793
  758.2 2.4 constant_dynamic-update-slice_fusion.61
  762.2 11.7 %cholesky.786 = f32[128,128]{1,0:T(8,128)S(1)} custom-call(f32[128,128]{1,0:T(8,128)S(1)} %cholesky.948), custom_call_target="Cholesky" | custom-call | tf_op jit(solution)/shard_map/jit(cholesky)/cholesky | solution.py:35
  775.8 9.9 custom-call.64
  789.1 11.7 %cholesky.807 = f32[128,128]{1,0:T(8,128)S(1)} custom-call(f32[128,128]{1,0:T(8,128)S(1)} %cholesky.953), custom_call_target="Cholesky" | custom-call | tf_op jit(solution)/shard_map/jit(cholesky)/cholesky | solution.py:35
  802.1 9.8 custom-call.65
  815.4 11.9 %cholesky.826 = f32[128,128]{1,0:T(8,128)S(1)} custom-call(f32[128,128]{1,0:T(8,128)S(1)} %cholesky.958), custom_call_target="Cholesky" | custom-call | tf_op jit(solution)/shard_map/jit(cholesky)/cholesky | solution.py:35
  828.6 9.8 custom-call.66
  841.9 11.7 %cholesky.845 = f32[128,128]{1,0:T(8,128)S(1)} custom-call(f32[128,128]{1,0:T(8,128)S(1)} %cholesky.963), custom_call_target="Cholesky" | custom-call | tf_op jit(solution)/shard_map/jit(cholesky)/cholesky | solution.py:35
  854.8 9.8 custom-call.67
  865.7 2.7 convolution_subtract_fusion.18
  868.4 11.7 %cholesky.864 = f32[128,128]{1,0:T(8,128)S(1)} custom-call(f32[128,128]{1,0:T(8,128)S(1)} %cholesky.968), custom_call_target="Cholesky" | custom-call | tf_op jit(solution)/shard_map/jit(cholesky)/cholesky | solution.py:35
  881.5 9.8 custom-call.68
  894.3 11.7 %cholesky.883 = f32[128,128]{1,0:T(8,128)S(1)} custom-call(f32[128,128]{1,0:T(8,128)S(1)} %cholesky.973), custom_call_target="Cholesky" | custom-call | tf_op jit(solution)/shard_map/jit(cholesky)/cholesky | solution.py:35
  907.3 10.0 custom-call.69
  919.9 11.7 %cholesky.900 = f32[128,128]{1,0:T(8,128)S(1)} custom-call(f32[128,128]{1,0:T(8,128)S(1)} %convolution_subtract_fusion.22), custom_call_target="Cholesky" | custom-call | tf_op jit(solution)/shard_map/jit(cholesky)/cholesky | solution.py:35
  937.8 4.9 select_select_fusion
  942.7 22.8 %while.5 = (s32[]{:T(128)}, f32[1024,1024]{1,0:T(8,128)}, s32[8,2]{0,1:T(2,128)S(1)}, f32[8,128,128]{2,1,0:T(8,128)S(1)}, s32[]{:T(128)}) while((s32[]{:T(128)}, f32[1024,1024]{1,0:T(8,128)}, s32[8,2]{0,1:T(2,128)S(1)}, f32[8,128,128]{2,1,0:T(8,128)S(1)}, s32[]{:T(128)}) %tuple.124), condition=%wide.while_cond.clone, body=%wide.while_body.clone.sunk | while | flops 2 | bytes 131181 | solution.py:36
  965.5 78.8 %custom-call.70 = f32[8,128,128]{1,2,0:T(8,128)S(1)} custom-call(f32[8,128,128]{2,1,0:T(8,128)S(1)} %get-tuple-element.22), custom_call_target="InvertDiagBlocksLowerTriangular" | custom-call | tf_op jit(solution)/shard_map/triangular_solve/custom-call.7 | solution.py:36
  1049.0 2.5 convolution_subtract_fusion.5
  1052.2 3.4 fusion.43
  1056.3 4.0 fusion.49
  1061.0 5.3 convolution_subtract_fusion.9
  1066.9 5.5 convolution_subtract_fusion.4
  1073.1 6.8 convolution_subtract_fusion.1
  1083.8 2.5 convolution_subtract_fusion.3
  1087.0 3.4 fusion.40
  1091.1 4.2 fusion.46
  1096.0 4.9 convolution_subtract_fusion.6
  1101.5 5.5 convolution_subtract_fusion.2
  1107.7 6.6 convolution_subtract_fusion
  1114.9 3.4 pad_maximum_fusion
  1118.4 8.0 copy.7
  (154 shorter events, 122.0 us)
Async XLA Ops:
  6.5 179.8 %reduce-scatter.3.cloned.1.call-start = ((), (), s32[]{:S(2)}) async-start(), calls=%async_computation.2 | async-start | bytes 11010048 | tf_op jit(solution)/shard_map/reduce_scatter | solution.py:31
  96.1 108.8 %reduce-scatter.5.cloned.1.call-start = ((), (), s32[]{:S(2)}) async-start(), calls=%async_computation.3 | async-start | bytes 11010048 | tf_op jit(solution)/shard_map/reduce_scatter | solution.py:31
  185.9 213.9 %all-reduce.4.cloned.1.call-start = ((), (), s32[]{:S(2)}) async-start(), calls=%async_computation.4 | async-start | bytes 16777216 | tf_op jit(solution)/shard_map/psum | solution.py:34
  421.1 1.9 copy-start
  1044.4 4.6 copy-start.2
  1072.5 8.1 copy-start.1
Sparse Core Ops, SparseCore 0:
  96.2 18.8 reduce-scatter.2
  186.0 18.8 reduce-scatter.4
  222.5 177.2 all-reduce.3
where the time goes:
time: 1150 us; the launch traced here: 1130 us
  other arithmetic  526 us (46%)
  matrix products  331 us (29%)
  waiting for transfers between devices  178 us (15%)
  local copies, waits for them, and re-layouts  72.2 us (6%)
  between operations  23.9 us (2%)
    another operation x62, other arithmetic, on_device(): factor = jnp.linalg.cholesky(gram_matrix)  345 us
    dot_general x2, matrix products, multiply(): jnp.dot(left_operand, right_operand, precision=lax.Precision.HIGHEST, pre...  179 us
    psum x1, waiting for transfers between devices, on_device(): gram_matrix = lax.psum(contract(row_product, row_product), ('row', 'col'))  177 us
    another operation x5, other arithmetic, on_device(): lax.linalg.triangular_solve(factor, row_product, left_side=False, lower=T...  167 us
    another operation x30, matrix products, on_device(): lax.linalg.triangular_solve(factor, row_product, left_side=False, lower=T...  70.3 us
    another operation x28, matrix products, on_device(): factor = jnp.linalg.cholesky(gram_matrix)  47 us
    another operation x51, local copies, waits for them, and re-layouts, on_device(): lax.linalg.triangular_solve(factor, row_product, left_side=False, lower=T...  45.5 us
    dot_general x2, matrix products, contract(): lax.dot_general(left_operand, right_operand, (((0,), (0,)), ((), ())), pr...  35 us
  transfers between devices with their start and end apart: 3, of which 2 were waited for; matrix products, arithmetic and copies ran while one was open for 9% of the time, Pallas kernels for 0%

commit v1 on v0

v1 whole, which is shorter than its diff:
```python
import jax
import jax.numpy as jnp
from jax import lax
from jax.experimental import pallas as pl
from jax.experimental.pallas import tpu as pltpu
from jax.sharding import PartitionSpec as P

B = 128
S = 8


def dot(left, right, dims):
    return lax.dot_general(
        left,
        right,
        (dims, ((), ())),
        precision=lax.Precision.HIGHEST,
        preferred_element_type=jnp.float32,
    )


def high(left, right, dims):
    return lax.dot_general(
        left,
        right,
        (dims, ((), ())),
        precision=lax.Precision.HIGH,
        preferred_element_type=jnp.float32,
    )


def invert_block(block):
    slabs = [block[S * g : S * (g + 1), :] for g in range(B // S)]
    lane = lax.broadcasted_iota(jnp.int32, (S, B), 1)
    sub = lax.broadcasted_iota(jnp.int32, (S, B), 0)
    for j in range(B):
        g, r = divmod(j, S)
        at_j = lane == j
        row = slabs[g][r : r + 1, :]
        scale = lax.rsqrt(jnp.broadcast_to(row[:, j : j + 1], (S, B)))
        done = jnp.where(at_j, 1.0, jnp.broadcast_to(row, (S, B))) * scale
        for h in range(g, B // S):
            slab = slabs[h]
            weight = jnp.broadcast_to(slab[:, j : j + 1], (S, B)) * scale
            new = jnp.where(at_j, 0.0, slab) - weight * done
            if h == g:
                new = jnp.where(sub > r, new, jnp.where(sub == r, done, slab))
            slabs[h] = new
    full = jnp.concatenate(slabs, axis=0)
    rows = lax.broadcasted_iota(jnp.int32, (B, B), 0)
    cols = lax.broadcasted_iota(jnp.int32, (B, B), 1)
    return jnp.where(cols <= rows, full, 0.0)


def inverse_kernel(gram_ref, out_ref, work, panel):
    size = gram_ref.shape[-1]
    blocks = size // B
    work[...] = gram_ref[0]
    col = lax.broadcasted_iota(jnp.int32, (B, size), 1)

    @pl.loop(0, blocks)
    def _(k):
        start = pl.multiple_of(k * B, B)
        here = pl.ds(start, B)
        inverse = invert_block(work[here, here])
        panel[...] = dot(inverse, work[here, :], ((1,), (0,)))
        panel[:, here] = inverse
        out_ref[0, here, :] = jnp.where(col < start + B, panel[...], 0.0)

        @pl.loop(k + 1, blocks)
        def _(i):
            rows = pl.ds(pl.multiple_of(i * B, B), B)
            work[rows, here] = jnp.zeros((B, B), jnp.float32)
            work[rows, :] -= dot(panel[:, rows], panel[...], ((0,), (0,)))


def inverse_factor(grams):
    count, size, _ = grams.shape
    spec = pl.BlockSpec((1, size, size), lambda m: (m, 0, 0))
    return pl.pallas_call(
        inverse_kernel,
        grid=(count,),
        out_shape=jax.ShapeDtypeStruct(grams.shape, jnp.float32),
        in_specs=[spec],
        out_specs=spec,
        scratch_shapes=[
            pltpu.VMEM((size, size), jnp.float32),
            pltpu.VMEM((B, size), jnp.float32),
        ],
        compiler_params=pltpu.CompilerParams(vmem_limit_bytes=40 * 2**20),
        cost_estimate=pl.CostEstimate(
            flops=count * size**3 * 12,
            bytes_accessed=count * size * size * 8,
            transcendentals=0,
        ),
    )(grams)


def on_device(statistic, eigenbasis):
    members = statistic.shape[0]
    cores = lax.axis_size("col")
    products, grams = [], []
    for member in range(members):
        product = lax.psum_scatter(
            high(statistic[member], eigenbasis[member], ((1,), (0,))),
            "col",
            scatter_dimension=0,
            tiled=True,
        )
        products.append(product)
        grams.append(high(product, product, ((0,), (0,))))
    grams = jnp.stack(grams)
    shared = members % cores == 0
    if shared:
        grams = lax.psum_scatter(grams, "col", scatter_dimension=0, tiled=True)
        grams = lax.psum(grams, "row")
    else:
        grams = lax.psum(grams, ("row", "col"))
    inverses = inverse_factor(grams)
    if shared:
        inverses = lax.all_gather(inverses, "col", axis=0, tiled=True)
    return jnp.stack(
        [high(products[m], inverses[m], ((1,), (1,))) for m in range(members)]
    )


def solution(mesh):
    placed = (P("layer", "row", "col"), P("layer", "col", None))
    return jax.shard_map(
        on_device,
        mesh=mesh,
        in_specs=placed,
        out_specs=P("layer", ("row", "col"), None),
        check_vma=False,
    )
```

time: 1150 us -> 528 us (0.46)
  other arithmetic: 526 us -> 8.52 us
  matrix products: 331 us -> 133 us
  Pallas kernels: 0 us -> 158 us
  local copies, waits for them, and re-layouts: 72.2 us -> 4.21 us
  waiting for transfers between devices: 178 us -> 203 us
    another operation x68 -> x2, other arithmetic: 516 us -> 8.52 us  [the longest x1 4.44 us: on_device(): jnp.stack([high(products[m], inverses[m], ((1,), (1,))) for m in range(me...]
    pallas_call x0 -> x1, Pallas kernels: none -> 158 us  [inverse_factor(): pl.pallas_call(inverse_kernel, grid=(count,), out_shape=jax.ShapeDtypeStr...]
    another operation x58 -> x0, matrix products: 117 us -> none  [the longest x30 70.3 us: on_device(): lax.linalg.triangular_solve(factor, row_product, left_side=False, lower=T...]
    dot_general x4 -> x6, matrix products: 214 us -> 133 us  [high(): lax.dot_general(left, right, (dims, ((), ())), precision=lax.Precision.HI...]
    another operation x68 -> x0, local copies, waits for them, and re-layouts: 59.4 us -> none  [the longest x51 45.5 us: on_device(): lax.linalg.triangular_solve(factor, row_product, left_side=False, lower=T...]
    reduce_scatter x2 -> x3, waiting for transfers between devices: 1.05 us -> 25.6 us  [the longest x1 17.8 us: on_device(): grams = lax.psum_scatter(grams, 'col', scatter_dimension=0, tiled=True)]
    psum x1, waiting for transfers between devices: 177 us -> 158 us  [on_device(): grams = lax.psum(grams, 'row')]
    all_gather x0 -> x1, waiting for transfers between devices: none -> 19 us  [on_device(): inverses = lax.all_gather(inverses, 'col', axis=0, tiled=True)]
  transfers between devices with their start and end apart: 3 -> 5, of which waited for: 2 -> 4; matrix products, arithmetic and copies ran while one was open for 9% -> 11% of each run, Pallas kernels for 0% -> 0%
where the time goes in v1:
time: 528 us; the launch traced here: 521 us
  waiting for transfers between devices  203 us (38%)
  Pallas kernels  158 us (30%)
  matrix products  133 us (25%)
  between operations  13.7 us (3%)
  other arithmetic  8.52 us (2%)
    pallas_call x1, Pallas kernels, inverse_factor(): pl.pallas_call(inverse_kernel, grid=(count,), out_shape=jax.ShapeDtypeStr...  158 us
    psum x1, waiting for transfers between devices, on_device(): grams = lax.psum(grams, 'row')  158 us
    dot_general x6, matrix products, high(): lax.dot_general(left, right, (dims, ((), ())), precision=lax.Precision.HI...  133 us
    all_gather x1, waiting for transfers between devices, on_device(): inverses = lax.all_gather(inverses, 'col', axis=0, tiled=True)  19 us
    reduce_scatter x1, waiting for transfers between devices, on_device(): grams = lax.psum_scatter(grams, 'col', scatter_dimension=0, tiled=True)  17.8 us
  transfers between devices with their start and end apart: 5, of which 4 were waited for; matrix products, arithmetic and copies ran while one was open for 11% of the time, Pallas kernels for 0%

profile of v1, /device:TPU:0, one launch (start us, length us, event | category | flops | bytes accessed | tf_op | source)
XLA Modules:
  0.0 521.1 jit_solution(129979519207107641)
XLA Ops:
  6.5 0.0 reduce-scatter.6.cloned.1.call-start
  6.5 47.7 %fusion = f32[1792,1024]{1,0:T(8,128)} fusion(f32[2,1792,3584]{2,1,0:T(8,128)} %param.2, f32[2,3584,1024]{2,1,0:T(8,128)} %param.3), kind=kOutput, calls=%fused_computation | convolution fusion | flops 39460012032 | bytes 47710208 | tf_op jit(solution)/shard_map/dot_general | solution.py:23
  54.2 0.0 reduce-scatter.6.cloned.1.call-update
  54.2 0.2 reduce-scatter.4.cloned.1.call-start
  54.5 47.7 %fusion.2 = f32[1792,1024]{1,0:T(8,128)} fusion(f32[2,1792,3584]{2,1,0:T(8,128)} %param.2, f32[2,3584,1024]{2,1,0:T(8,128)} %param.3), kind=kOutput, calls=%fused_computation.2 | convolution fusion | flops 39460012032 | bytes 47710208 | tf_op jit(solution)/shard_map/dot_general | solution.py:23
  102.1 0.0 reduce-scatter.4.cloned.1.call-update
  102.1 0.3 reduce-scatter.8.cloned.1.call-start
  102.4 0.0 reduce-scatter.6.cloned.1.call-done
  102.4 10.9 %convolution_bitcast_fusion = f32[1,1024,1024]{2,1,0:T(8,128)} fusion(f32[896,1024]{1,0:T(8,128)} %reduce-scatter.6.cloned.1.call-done), kind=kOutput, calls=%fused_computation.16 | convolution fusion | flops 5637144576 | bytes 7864320 | tf_op jit(solution)/shard_map/dot_general | solution.py:23
  113.3 7.8 %reduce-scatter.4.cloned.1.call-done = f32[896,1024]{1,0:T(8,128)} async-done(((f32[1792,1024]{1,0:T(8,128)}), f32[896,1024]{1,0:T(8,128)}) %reduce-scatter.4.cloned.1.call-update) | async-done | bytes 3670032 | tf_op jit(solution)/shard_map/reduce_scatter | solution.py:104
  121.1 0.0 copy-start.2
  121.1 10.5 %convolution_bitcast_fusion.1 = f32[1,1024,1024]{2,1,0:T(8,128)S(1)} fusion(f32[896,1024]{1,0:T(8,128)} %reduce-scatter.4.cloned.1.call-done), kind=kOutput, calls=%fused_computation.17 | convolution fusion | flops 5637144576 | bytes 7864320 | tf_op jit(solution)/shard_map/dot_general | solution.py:23
  131.7 0.0 copy-done.2
  131.7 4.1 pad_maximum_fusion
  135.8 0.0 reduce-scatter.8.cloned.1.call-update
  135.8 0.0 all-reduce.2.cloned.1.call-start
  135.8 17.8 %reduce-scatter.8.cloned.1.call-done = f32[1,1024,1024]{2,1,0:T(8,128)} async-done(((f32[2,1024,1024]{2,1,0:T(8,128)}), f32[1,1024,1024]{2,1,0:T(8,128)}) %reduce-scatter.8.cloned.1.call-update) | async-done | bytes 4194320 | tf_op jit(solution)/shard_map/reduce_scatter | solution.py:115
  153.6 0.0 all-reduce.2.cloned.1.call-update
  153.6 0.3 all-gather.2.cloned.1.call-start
  153.9 158.2 %all-reduce.2.cloned.1.call-done.gram_ref = f32[1,1024,1024]{2,1,0:T(8,128)} async-done(((f32[1,1024,1024]{2,1,0:T(8,128)}), f32[1,1024,1024]{2,1,0:T(8,128)}) %all-reduce.2.cloned.1.call-update) | async-done | bytes 4194320 | tf_op jit(solution)/shard_map/psum | solution.py:116
  312.1 0.0 copy-start.1
  312.1 2.2 copy-done.1
  314.3 158.5 %shard_map.28 = f32[1,1024,1024]{2,1,0:T(8,128)S(1)} custom-call(f32[1,1024,1024]{2,1,0:T(8,128)S(1)} %copy-done.1), custom_call_target="tpu_custom_call" | custom-call | flops 12884901888 | bytes 8388608 | tf_op jit(solution)/shard_map/pallas_call | solution.py:80
  472.8 0.0 copy-start
  472.8 2.0 copy-done
  474.8 0.0 all-gather.2.cloned.1.call-update
  474.8 19.0 %all-gather.2.cloned.1.call-done = f32[2,1024,1024]{2,1,0:T(8,128)} async-done(((f32[1,1024,1024]{2,1,0:T(8,128)}), f32[2,1024,1024]{2,1,0:T(8,128)}) %all-gather.2.cloned.1.call-update) | async-done | bytes 8388624 | tf_op jit(solution)/shard_map/all_gather | solution.py:121
  493.8 0.0 copy-start.3
  493.8 0.0 copy-start.4
  493.8 9.9 %fusion.13 = f32[1,896,1024]{2,1,0:T(8,128)S(1)} fusion(f32[896,1024]{1,0:T(8,128)} %reduce-scatter.6.cloned.1.call-done, f32[2,1024,1024]{2,1,0:T(8,128)} %all-gather.2.cloned.1.call-done), kind=kOutput, calls=%fused_computation.19 | convolution fusion | flops 5637144576 | bytes 11534336 | tf_op jit(solution)/shard_map/dot_general | solution.py:23
  503.7 0.0 copy-done.3
  503.7 0.0 copy-done.4
  503.7 5.9 %fusion.12 = f32[1,896,1024]{2,1,0:T(8,128)S(1)} fusion(f32[896,1024]{1,0:T(8,128)S(1)} %copy-done.4, f32[2,1024,1024]{2,1,0:T(8,128)S(1)} %copy-done.3), kind=kOutput, calls=%fused_computation.18 | convolution fusion | flops 5637144576 | bytes 11534336 | tf_op jit(solution)/shard_map/dot_general | solution.py:23
  509.6 4.4 pad_maximum_fusion.1
Async XLA Ops:
  6.5 95.9 %reduce-scatter.6.cloned.1.call-start = ((), (), s32[]{:S(2)}) async-start(), calls=%async_computation.4 | async-start | bytes 11010048 | tf_op jit(solution)/shard_map/reduce_scatter | solution.py:104
  54.2 66.9 %reduce-scatter.4.cloned.1.call-start = ((), (), s32[]{:S(2)}) async-start(), calls=%async_computation.3 | async-start | bytes 11010048 | tf_op jit(solution)/shard_map/reduce_scatter | solution.py:104
  102.1 51.5 %reduce-scatter.8.cloned.1.call-start = ((), (), s32[]{:S(2)}) async-start(), calls=%async_computation.5 | async-start | bytes 12582912 | tf_op jit(solution)/shard_map/reduce_scatter | solution.py:115
  121.1 10.5 %copy-start.2 = (f32[1,1024,1024]{2,1,0:T(8,128)S(1)}, f32[1,1024,1024]{2,1,0:T(8,128)}, u32[]{:S(2)}) copy-start(f32[1,1024,1024]{2,1,0:T(8,128)} %convolution_bitcast_fusion) | copy-start | bytes 12582916
  135.8 176.3 %all-reduce.2.cloned.1.call-start = ((), (), s32[]{:S(2)}) async-start(), calls=%async_computation.6 | async-start | bytes 8388608 | tf_op jit(solution)/shard_map/psum | solution.py:116
  153.6 340.2 %all-gather.2.cloned.1.call-start = ((), (), s32[]{:S(2)}) async-start(), calls=%async_computation.7 | async-start | bytes 12582912 | tf_op jit(solution)/shard_map/all_gather | solution.py:121
  312.1 2.2 copy-start.1
  472.8 2.0 copy-start
  493.8 9.9 %copy-start.3 = (f32[2,1024,1024]{2,1,0:T(8,128)S(1)}, f32[2,1024,1024]{2,1,0:T(8,128)}, u32[]{:S(2)}) copy-start(f32[2,1024,1024]{2,1,0:T(8,128)} %all-gather.2.cloned.1.call-done) | copy-start | bytes 25165828
  493.8 9.9 %copy-start.4 = (f32[896,1024]{1,0:T(8,128)S(1)}, f32[896,1024]{1,0:T(8,128)}, u32[]{:S(2)}) copy-start(f32[896,1024]{1,0:T(8,128)} %reduce-scatter.4.cloned.1.call-done) | copy-start | bytes 11010052
Sparse Core Ops, SparseCore 0:
  54.4 18.8 reduce-scatter.5
  102.3 18.8 reduce-scatter.3
  135.9 17.6 reduce-scatter.7
  155.8 156.2 all-reduce.1
  475.0 18.8 all-gather.1
